TPU v7x, 1024 devices: a whole 4x8x16 slice. The times are simulated.
1024 devices in a mesh: dp: 16 (over z_hi, x, core), expert: 64 (over z_lo, y).
Axes of the slice: x: 4, y: 8, z: 16 (z_hi: 2, z_lo: 8; z = z_hi * 8 + z_lo), core: 2. Of those that a mesh axis runs over, the one named last changes fastest.
Arguments:
- tokens: bfloat16 [131072, 2048], P(('dp', 'expert')), may hold values from -6 to 6
- expert_ids: int32 [131072, 2], P(('dp', 'expert')), may hold values from 0 to 63, as said below
- gate_values: float32 [131072, 2], P(('dp', 'expert')), may hold values from 0.25 to 1
- capacity: int32 [32], replicated, may hold values from 2 to 4, as said below
- w_in: bfloat16 [64, 2048, 1024], P('expert', 'dp'), may hold values from -0.125 to 0.125
- w_down: bfloat16 [64, 512, 2048], P('expert', None, 'dp'), may hold values from -0.1875 to 0.1875
Outputs:
- mixed: bfloat16 [131072, 2048], P(('dp', 'expert'))
Inputs may be any that keep to these rules, and one draw needn't show every extreme that they name: `expert_ids`: A token's two ids differ. One expert, the busy one, has capacity 4 and is named by the first 4 tokens of every source. The busy expert's capacity is 4.
All inputs are finite; a program needn't handle non-finite values.
Results may differ from a plain program's by a relative error of at most 0.0065.
Values may be sent and summed in bfloat16 or wider, within the bound.
A program may use at most 32 MiB of HBM per device.

v0:
```python
import jax
import jax.numpy as jnp
from jax import lax
from jax.sharding import PartitionSpec as P

CAP = 4


def per_device(tokens, expert_ids, gate_values, capacity, w_in, w_down):
    tok_count = tokens.shape[0]
    width = tokens.shape[1]
    window = capacity.shape[0]
    flat_ids = expert_ids.reshape(-1)
    expert_range = jnp.arange(window, dtype=jnp.int32)
    one_hot = (flat_ids[:, None] == expert_range[None, :]).astype(jnp.int32)
    slot_rank = jnp.sum((jnp.cumsum(one_hot, axis=0) - one_hot) * one_hot, axis=1)
    slot_limit = jnp.sum(one_hot * capacity[None, :], axis=1)
    kept_mask = (jnp.sum(one_hot, axis=1) > 0) & (slot_rank < slot_limit)
    slot_index = flat_ids * CAP + slot_rank
    slot_range = jnp.arange(window * CAP, dtype=jnp.int32)
    slot_select = ((slot_index[None, :] == slot_range[:, None]) & kept_mask[None, :]).astype(
        jnp.float32
    )
    select_tokens = slot_select.reshape(window * CAP, tok_count, 2).sum(axis=2)
    slot_weights = (
        (slot_select * gate_values.reshape(-1)[None, :])
        .reshape(window * CAP, tok_count, 2)
        .sum(axis=2)
    )
    outgoing = jnp.dot(
        select_tokens.astype(jnp.bfloat16), tokens, preferred_element_type=jnp.float32
    ).astype(jnp.bfloat16)
    doubled = jnp.broadcast_to(outgoing.reshape(window, 1, CAP, width), (window, 2, CAP, width))
    received = lax.all_to_all(
        doubled.reshape(2 * window, CAP, width), "expert", split_axis=0, concat_axis=0, tiled=True
    )
    token_rows = received.reshape(-1, width)
    local_in = w_in[0]
    local_down = w_down[0]
    half_width = local_in.shape[1] // 2
    gate_up = jnp.dot(
        token_rows,
        lax.all_gather(local_in, "dp", axis=0, tiled=True),
        preferred_element_type=jnp.float32,
    )
    hidden = (jax.nn.silu(gate_up[:, :half_width]) * gate_up[:, half_width:]).astype(jnp.bfloat16)
    partial_value = jnp.dot(
        hidden,
        lax.all_gather(local_down, "dp", axis=1, tiled=True),
        preferred_element_type=jnp.float32,
    ).astype(jnp.bfloat16)
    partial_value = partial_value.reshape(2 * window, CAP, width)
    returned = lax.all_to_all(partial_value, "expert", split_axis=0, concat_axis=0, tiled=True)
    returned = returned.reshape(window, 2, CAP, width).astype(jnp.float32)
    summed = (returned[:, 0] + returned[:, 1]).astype(jnp.bfloat16)
    summed = lax.optimization_barrier(summed)
    combined = summed.reshape(window * CAP, width).astype(jnp.float32)
    mixed = jnp.einsum(
        "st,sd->td",
        slot_weights,
        combined,
        precision=lax.Precision.HIGHEST,
        preferred_element_type=jnp.float32,
    )
    return mixed.astype(jnp.bfloat16)


def solution(mesh):
    return jax.shard_map(
        per_device,
        mesh=mesh,
        in_specs=(
            P(("dp", "expert"), None),
            P(("dp", "expert"), None),
            P(("dp", "expert"), None),
            P(),
            P("expert", "dp", None),
            P("expert", None, "dp"),
        ),
        out_specs=P(("dp", "expert"), None),
        check_vma=False,
    )
```

profile of v0, /device:TPU:1, one launch (start us, length us, event | category | flops | bytes accessed | tf_op | source)
XLA Modules:
  0.0 332.9 jit_solution(610456627780098649)
XLA Ops:
  6.5 0.0 copy-start
  6.5 0.0 all-gather.5.cloned.1.call-start
  6.5 0.7 all-gather.5.cloned.1.call-update
  7.3 0.8 copy.23
  8.0 0.1 eq.44
  8.2 0.1 eq.40
  8.3 0.6 reduce-window.6
  8.9 0.2 slice_reduce_fusion
  9.2 0.8 select_reduce_fusion.1
  9.9 0.1 reduce_sum.50
  10.1 0.1 reduce_sum.53
  10.2 0.2 gt.15
  10.4 0.1 copy.26
  10.5 0.1 copy.27
  10.6 0.7 multiply_add_fusion
  11.3 0.7 convert_reduce_fusion
  12.0 0.0 copy-done
  12.0 0.3 convolution_convert_fusion.2
  12.3 0.2 broadcast_in_dim.4
  12.5 1.6 broadcast_in_dim.5
  14.1 22.5 %all-to-all-start = ((bf16[64,4,2048]{2,1,0:T(4,128)(2,1)}), bf16[64,4,2048]{2,1,0:T(4,128)(2,1)S(1)}, u32[]{:S(2)}, u32[]{:S(2)}) async-start(bf16[64,4,2048]{2,1,0:T(4,128)(2,1)} %bitcast.1), calls=%async_computation | async-start | bytes 2097152 | tf_op jit(solution)/shard_map/all_to_all | solution.py:34
  36.6 0.0 all-gather.7.cloned.1.call-start
  36.7 0.7 all-gather.7.cloned.1.call-update
  37.4 61.6 %all-to-all-done = bf16[64,4,2048]{2,1,0:T(4,128)(2,1)S(1)} async-done(((bf16[64,4,2048]{2,1,0:T(4,128)(2,1)}), bf16[64,4,2048]{2,1,0:T(4,128)(2,1)S(1)}, u32[]{:S(2)}, u32[]{:S(2)}) %all-to-all-start) | async-done | bytes 1048608 | tf_op jit(solution)/shard_map/all_to_all | solution.py:34
  99.0 0.3 reshape.96
  99.3 71.4 %all-gather.5.cloned.1.call-done = bf16[1,2048,1024]{2,1,0:T(8,128)(2,1)} async-done(((bf16[1,128,1024]{2,1,0:T(8,128)(2,1)}), bf16[1,2048,1024]{2,1,0:T(8,128)(2,1)}) %all-gather.5.cloned.1.call-update) | async-done | bytes 4194320 | tf_op jit(solution)/shard_map/all_gather | solution.py:43
  170.7 3.4 %fusion = f32[256,1024]{1,0:T(8,128)S(1)} fusion(bf16[256,2048]{1,0:T(8,128)(2,1)S(1)} %reshape.96, bf16[1,2048,1024]{2,1,0:T(8,128)(2,1)} %all-gather.5.cloned.1.call-done), kind=kOutput, calls=%fused_computation | convolution fusion | flops 1073741824 | bytes 6291456 | tf_op jit(solution)/shard_map/dot_general | solution.py:41
  174.1 88.3 %all-gather.7.cloned.1.call-done = bf16[1,512,2048]{2,1,0:T(8,128)(2,1)} async-done(((bf16[1,512,128]{2,1,0:T(8,128)(2,1)}), bf16[1,512,2048]{2,1,0:T(8,128)(2,1)}) %all-gather.7.cloned.1.call-update) | async-done | bytes 2097168 | tf_op jit(solution)/shard_map/all_gather | solution.py:49
  262.4 2.3 convolution_convert_fusion
  264.7 0.4 reshape.97
  265.2 58.8 %all_to_all.10 = bf16[64,4,2048]{2,1,0:T(4,128)(2,1)S(1)} all-to-all(bf16[64,4,2048]{2,1,0:T(4,128)(2,1)S(1)} %reshape.97), channel_id=1, replica_groups=mesh['dp'=16,'expert'=64] {'expert'}, dimensions={0} | all-to-all | bytes 2097152 | tf_op jit(solution)/shard_map/all_to_all | solution.py:53
  323.9 0.2 convert.1
  324.2 0.3 fusion.4
  324.5 0.1 reshape.98
  324.6 1.4 convolution_convert_fusion.1
  (5 shorter events, 0.1 us)
Async XLA Ops:
  6.5 5.5 %copy-start = (bf16[128,2048]{1,0:T(8,128)(2,1)S(1)}, bf16[128,2048]{1,0:T(8,128)(2,1)}, u32[]{:S(2)}) copy-start(bf16[128,2048]{1,0:T(8,128)(2,1)} %param.6) | copy-start | bytes 1572868
  6.5 164.1 %all-gather.5.cloned.1.call-start = ((), (), s32[]{:S(2)}) async-start(), calls=%async_computation.2 | async-start | bytes 4456448 | tf_op jit(solution)/shard_map/all_gather | solution.py:43
  14.1 84.9 %all-to-all-start = ((bf16[64,4,2048]{2,1,0:T(4,128)(2,1)}), bf16[64,4,2048]{2,1,0:T(4,128)(2,1)S(1)}, u32[]{:S(2)}, u32[]{:S(2)}) async-start(bf16[64,4,2048]{2,1,0:T(4,128)(2,1)} %bitcast.1), calls=%async_computation | async-start | bytes 2097152 | tf_op jit(solution)/shard_map/all_to_all | solution.py:34
  36.6 225.8 %all-gather.7.cloned.1.call-start = ((), (), s32[]{:S(2)}) async-start(), calls=%async_computation.3 | async-start | bytes 2228224 | tf_op jit(solution)/shard_map/all_gather | solution.py:49
Sparse Core Ops, SparseCore 0:
  11.8 158.7 all-gather.4
  175.0 87.3 all-gather.6
where the time goes:
time: 334 us; the launch traced here: 333 us
  waiting for transfers between devices  223 us (67%)
  blocking collectives  58.8 us (18%)
  starting transfers between devices  22.6 us (7%)
  between operations  13.5 us (4%)
  matrix products  7.46 us (2%)
  local copies, waits for them, and re-layouts  4.4 us (1%)
  other arithmetic  3.43 us (1%)
    all_gather x1, waiting for transfers between devices, per_device(): lax.all_gather(local_down, 'dp', axis=1, tiled=True)  88.3 us
    all_gather x1, waiting for transfers between devices, per_device(): lax.all_gather(local_in, 'dp', axis=0, tiled=True)  71.4 us
    all_to_all x1, waiting for transfers between devices, per_device(): lax.all_to_all(doubled.reshape(2 * window, CAP, width), 'expert', split_a...  61.6 us
    all_to_all x1, blocking collectives, per_device(): lax.all_to_all(partial_value, 'expert', split_axis=0, concat_axis=0, tile...  58.8 us
    all_to_all x1, starting transfers between devices, per_device(): lax.all_to_all(doubled.reshape(2 * window, CAP, width), 'expert', split_a...  22.5 us
  transfers between devices with their start and end apart: 3, of which 3 were waited for; matrix products, arithmetic and copies ran while one was open for 3% of the time, Pallas kernels for 0%

commit v1 on v0

v1 whole, which is shorter than its diff:
```python
import jax
import jax.numpy as jnp
from jax import lax
from jax.experimental import pallas as pl
from jax.experimental.pallas import tpu as pltpu
from jax.sharding import PartitionSpec as P

NX = 4
NC = 2
ZL = 8
NY = 8
NK = NY // 2
ZBLK = 16
YBLK = 32
MESH = pl.DeviceIdType.MESH
BF = jnp.bfloat16
F32 = jnp.float32


def mo(value, multiple):
    return pl.multiple_of(value, multiple)


def layer_kernel(
    tok_hbm, ids_ref, gate_ref, cap_ref, win_hbm, wdn_hbm, out_ref,
    tok, slots_out, slots_z, slots_y, rows, w_in, w_down, relay_in, relay_down,
    acc, hidden, partial, from_y, to_z, from_z, mix,
    load_sem, z1_send, z1_recv, y1_send, y1_recv, w_send, w_recv, relay_recv,
    y2_send, y2_recv, z2_send, z2_recv,
):
    dp = lax.axis_index("dp")
    ex = lax.axis_index("expert")
    zh = dp // (NX * NC)
    xi = (dp // NC) % NX
    core = dp % NC
    zl = ex // NY
    yi = ex % NY

    def dp_of(h, x, c):
        return h * (NX * NC) + x * NC + c

    sibling = (dp_of(zh, xi, 1 - core), ex)
    x_up = (xi + 1) % NX
    x_down = (xi + NX - 1) % NX
    dev_up = (dp_of(zh, x_up, core), ex)
    dev_down = (dp_of(zh, x_down, core), ex)
    sign = 1 - 2 * core
    z_all = zh * ZL + zl
    z_next = (z_all + (ZL // 2) * sign + 2 * ZL) % (2 * ZL)
    dev_relay = (dp_of(z_next // ZL, xi, core), (z_next % ZL) * NY + yi)
    z_prev = (z_all - (ZL // 2) * sign + 2 * ZL) % (2 * ZL)
    relay_slot = dp_of(z_prev // ZL, xi, core)
    dev_cross = (dp_of(1 - zh, xi, core), ((zl + ZL // 2) % ZL) * NY + yi)

    def dev_z(z):
        return (dp, z * NY + yi)

    def dev_y(y):
        return (dp, zl * NY + y)

    barrier = pltpu.get_barrier_semaphore()
    for peer in (sibling, dev_up, dev_down, dev_cross):
        pl.semaphore_signal(barrier, inc=1, device_id=peer, device_id_type=MESH)

    def greet(d, carry):
        pl.semaphore_signal(barrier, inc=1, device_id=dev_y((yi + d) % NY), device_id_type=MESH)
        pl.semaphore_signal(barrier, inc=1, device_id=dev_z((zl + d) % ZL), device_id_type=MESH)
        return carry

    lax.fori_loop(1, ZL, greet, 0)

    load_tok = pltpu.make_async_copy(tok_hbm, tok, load_sem.at[0])
    load_in = pltpu.make_async_copy(
        win_hbm, w_in.at[pl.ds(mo(dp * 128, 128), 128), :], load_sem.at[1]
    )
    load_down = pltpu.make_async_copy(wdn_hbm, w_down.at[dp], load_sem.at[2])
    load_in.start()
    load_tok.start()
    load_down.start()

    row = lax.broadcasted_iota(jnp.int32, (128, 128), 0)
    col = lax.broadcasted_iota(jnp.int32, (128, 128), 1)
    expert = row >> 2
    slot = row & 3
    first = ids_ref[0:1, :] == expert
    second = ids_ref[1:2, :] == expert
    named = jnp.where(first, 1.0, 0.0) + jnp.where(second, 1.0, 0.0)
    before = jnp.where(row < col, 1.0, 0.0).astype(BF)
    rank = jnp.dot(named.astype(BF), before, preferred_element_type=F32)
    wide_row = lax.broadcasted_iota(jnp.int32, (128, 32), 0)
    wide_col = lax.broadcasted_iota(jnp.int32, (128, 32), 1)
    cap_col = jnp.sum(
        jnp.where((wide_row >> 2) == wide_col, cap_ref[0:1, :].astype(F32), 0.0),
        axis=1,
        keepdims=True,
    )
    slot_f = slot.astype(F32)
    kept = (rank == slot_f) & (slot_f < cap_col)
    take_first = kept & first
    take_second = kept & second
    select = (jnp.where(take_first, 1.0, 0.0) + jnp.where(take_second, 1.0, 0.0)).astype(BF)
    weight = jnp.where(take_first, gate_ref[0:1, :], 0.0) + jnp.where(
        take_second, gate_ref[1:2, :], 0.0
    )
    weight = weight.T
    for part in range(3):
        piece_w = weight.astype(BF)
        mix[part] = piece_w
        weight = weight - piece_w.astype(F32)
    load_tok.wait()
    slots_out[...] = jnp.dot(select, tok[...], preferred_element_type=F32).astype(BF)
    to_pairs = ((((row >> 2) & 7) * 16 + (row >> 5) * 4 + (row & 3)) == col)
    to_pairs = jnp.where(to_pairs, 1.0, 0.0).astype(BF)
    to_lines = ((((row >> 2) & 3) * 32 + (row >> 4) * 4 + (row & 3)) == col)
    to_lines = jnp.where(to_lines, 1.0, 0.0).astype(BF)

    load_in.wait()
    load_down.wait()
    pl.semaphore_wait(barrier, 4 + 2 * (ZL - 1))

    sends = []

    def piece(p, i):
        if p == 2:
            return w_down.at[i]
        return w_in.at[pl.ds(mo(i * 128 + 64 * p, 64), 64), :]

    def relay_piece(p):
        if p == 2:
            return relay_down
        return relay_in.at[pl.ds(64 * p, 64), :]

    counter = [0, 0, 0]

    def send_to(p, src, dst, recv, dev):
        k = counter[p]
        counter[p] += 1
        copy = pltpu.make_async_remote_copy(
            src_ref=src, dst_ref=dst, send_sem=w_send.at[p, k], recv_sem=recv,
            device_id=dev, device_id_type=MESH,
        )
        copy.start()
        sends.append(copy)

    def send_piece(p, i, dev):
        send_to(p, piece(p, i), piece(p, i), w_recv.at[p, i], dev)

    def wait_piece(p, i):
        pltpu.make_async_remote_copy(
            src_ref=piece(p, i), dst_ref=piece(p, i), send_sem=w_send.at[p, 0],
            recv_sem=w_recv.at[p, i], device_id=sibling, device_id_type=MESH,
        ).wait_recv()

    def send_own(p, h):
        i = dp_of(h, xi, core)
        send_piece(p, i, dev_up)
        send_piece(p, i, dev_down)
        send_piece(p, i, sibling)

    def send_relay(p):
        send_to(p, piece(p, dp), relay_piece(p), relay_recv.at[p], dev_relay)

    def pass_relay(p):
        pltpu.make_async_remote_copy(
            src_ref=relay_piece(p), dst_ref=relay_piece(p), send_sem=w_send.at[p, 0],
            recv_sem=relay_recv.at[p], device_id=sibling, device_id_type=MESH,
        ).wait_recv()
        send_to(p, relay_piece(p), piece(p, relay_slot), w_recv.at[p, relay_slot], dev_relay)

    def pass_near(p, h):
        step = 1 - 2 * ((core + p) % 2)
        src_x = (xi - step + NX) % NX
        dst_x = (xi + step + NX) % NX
        i = dp_of(h, src_x, core)
        wait_piece(p, i)
        send_piece(p, i, (dp_of(zh, dst_x, core), ex))
        send_piece(p, i, sibling)
        i = dp_of(h, dst_x, core)
        wait_piece(p, i)
        send_piece(p, i, sibling)

    def pass_far(p, h):
        i = dp_of(h, (xi + 2) % NX, core)
        wait_piece(p, i)
        send_piece(p, i, sibling)

    def wait_sibling(p, h):
        for j in range(NX):
            wait_piece(p, dp_of(h, (xi + j) % NX, 1 - core))

    def block_cols(h):
        return pl.ds(mo(((zh + h) % 2) * 1024, 1024), 1024)

    def z1_copy(h, d):
        z = (zl + d) % ZL
        return pltpu.make_async_remote_copy(
            src_ref=slots_out.at[pl.ds(mo(z * ZBLK, ZBLK), ZBLK), block_cols(h)],
            dst_ref=slots_z.at[pl.ds(mo(zl * ZBLK, ZBLK), ZBLK), block_cols(h)],
            send_sem=z1_send.at[h, d], recv_sem=z1_recv.at[h, zl],
            device_id=dev_z(z), device_id_type=MESH,
        )

    def z1_wait(h, d):
        z = (zl + d) % ZL
        pltpu.make_async_remote_copy(
            src_ref=slots_out.at[pl.ds(mo(z * ZBLK, ZBLK), ZBLK), block_cols(h)],
            dst_ref=slots_z.at[pl.ds(mo(z * ZBLK, ZBLK), ZBLK), block_cols(h)],
            send_sem=z1_send.at[h, d], recv_sem=z1_recv.at[h, z],
            device_id=dev_z(z), device_id_type=MESH,
        ).wait_recv()

    def y1_copy(h, d):
        y = (yi + d) % NY
        return pltpu.make_async_remote_copy(
            src_ref=slots_y.at[pl.ds(mo((y // 2) * YBLK, YBLK), YBLK), block_cols(h)],
            dst_ref=rows.at[pl.ds(mo(yi * YBLK, YBLK), YBLK), block_cols(h)],
            send_sem=y1_send.at[h, d], recv_sem=y1_recv.at[h, yi],
            device_id=dev_y(y), device_id_type=MESH,
        )

    def y1_wait(h, d):
        y = (yi + d) % NY
        pltpu.make_async_remote_copy(
            src_ref=slots_y.at[pl.ds(mo((y // 2) * YBLK, YBLK), YBLK), block_cols(h)],
            dst_ref=rows.at[pl.ds(mo(y * YBLK, YBLK), YBLK), block_cols(h)],
            send_sem=y1_send.at[h, d], recv_sem=y1_recv.at[h, y],
            device_id=dev_y(y), device_id_type=MESH,
        ).wait_recv()

    def chunk_slot(j):
        return ((zh + j // 2) % 2) * 8 + ((xi // 2 + j) % 2) * 4

    def chunk_cols(j):
        return pl.ds(mo(chunk_slot(j) * 128, 512), 512)

    def y2_copy(j, d):
        y = (yi + d) % NY
        return pltpu.make_async_remote_copy(
            src_ref=partial.at[pl.ds(mo(y * YBLK, YBLK), YBLK), chunk_cols(j)],
            dst_ref=from_y.at[pl.ds(mo(yi * YBLK, YBLK), YBLK), chunk_cols(j)],
            send_sem=y2_send.at[j, d], recv_sem=y2_recv.at[j, yi],
            device_id=dev_y(y), device_id_type=MESH,
        )

    def y2_wait(j, d):
        y = (yi + d) % NY
        pltpu.make_async_remote_copy(
            src_ref=partial.at[pl.ds(mo(y * YBLK, YBLK), YBLK), chunk_cols(j)],
            dst_ref=from_y.at[pl.ds(mo(y * YBLK, YBLK), YBLK), chunk_cols(j)],
            send_sem=y2_send.at[j, d], recv_sem=y2_recv.at[j, y],
            device_id=dev_y(y), device_id_type=MESH,
        ).wait_recv()

    def z2_copy(j, d):
        z = (zl + d) % ZL
        return pltpu.make_async_remote_copy(
            src_ref=to_z.at[pl.ds(mo(z * ZBLK, ZBLK), ZBLK), chunk_cols(j)],
            dst_ref=from_z.at[pl.ds(mo(zl * ZBLK, ZBLK), ZBLK), chunk_cols(j)],
            send_sem=z2_send.at[j, d], recv_sem=z2_recv.at[j, zl],
            device_id=dev_z(z), device_id_type=MESH,
        )

    def z2_wait(j, d):
        z = (zl + d) % ZL
        pltpu.make_async_remote_copy(
            src_ref=to_z.at[pl.ds(mo(z * ZBLK, ZBLK), ZBLK), chunk_cols(j)],
            dst_ref=from_z.at[pl.ds(mo(z * ZBLK, ZBLK), ZBLK), chunk_cols(j)],
            send_sem=z2_send.at[j, d], recv_sem=z2_recv.at[j, z],
            device_id=dev_z(z), device_id_type=MESH,
        ).wait_recv()

    def start_all(make, h):
        def body(d, carry):
            make(h, d).start()
            return carry

        lax.fori_loop(1, ZL, body, 0)

    def sent_all(make, h):
        def body(d, carry):
            make(h, d).wait_send()
            return carry

        lax.fori_loop(1, ZL, body, 0)

    def wait_all(wait, h):
        def body(d, carry):
            wait(h, d)
            return carry

        lax.fori_loop(1, ZL, body, 0)

    own_z = pl.ds(mo(zl * ZBLK, ZBLK), ZBLK)
    own_y = pl.ds(mo(yi * YBLK, YBLK), YBLK)
    own_pair = pl.ds(mo((yi // 2) * YBLK, YBLK), YBLK)

    for p in (0, 1):
        send_relay(p)
        send_own(p, zh)
    for h in (0, 1):
        start_all(z1_copy, h)
        slots_z[own_z, block_cols(h)] = slots_out[own_z, block_cols(h)]
    send_relay(2)
    send_own(2, zh)

    def spread(h):
        wait_all(z1_wait, h)
        slots_y[:, block_cols(h)] = jnp.dot(
            to_pairs, slots_z[:, block_cols(h)], preferred_element_type=F32
        ).astype(BF)
        start_all(y1_copy, h)
        rows[own_y, block_cols(h)] = slots_y[own_pair, block_cols(h)]

    zo = 1 - zh
    pass_near(0, zh)
    pass_near(1, zh)
    pass_relay(0)
    pass_relay(1)
    spread(0)
    pass_far(0, zh)
    pass_far(1, zh)
    pass_near(2, zh)
    spread(1)
    pass_relay(2)
    pass_far(2, zh)
    for p in (0, 1):
        i = dp_of(zo, xi, core)
        wait_piece(p, i)
        send_own(p, zo)
    pass_near(0, zo)
    pass_near(1, zo)

    def gate_up(h):
        def body(j, carry):
            m = ((zh + h) % 2) * NX + (xi + j) % NX
            at = pl.ds(mo(m * 256, 256), 256)
            product = jnp.dot(rows[:, at], w_in[at, :], preferred_element_type=F32)
            acc[...] = acc[...] + product
            return carry

        lax.fori_loop(0, NX, body, 0)

    acc[...] = jnp.zeros_like(acc)
    wait_all(y1_wait, 0)
    wait_sibling(0, zh)
    wait_sibling(1, zh)
    gate_up(0)
    i = dp_of(zo, xi, core)
    wait_piece(2, i)
    send_own(2, zo)
    pass_far(0, zo)
    pass_far(1, zo)
    pass_near(2, zo)
    wait_all(y1_wait, 1)
    wait_sibling(0, zo)
    wait_sibling(1, zo)
    gate_up(1)
    gate = acc[:, 0:512]
    small = jnp.exp(-jnp.abs(gate))
    gated = gate * jnp.where(gate >= 0, 1.0, small) / (1.0 + small)
    hidden[...] = (gated * acc[:, 512:1024]).astype(BF)

    def down(j):
        i = chunk_slot(j)
        weights = jnp.concatenate([w_down[i + q] for q in range(4)], axis=1)
        partial[:, chunk_cols(j)] = jnp.dot(
            hidden[...], weights, preferred_element_type=F32
        ).astype(BF)
        start_all(y2_copy, j)
        from_y[own_y, chunk_cols(j)] = partial[own_y, chunk_cols(j)]

    def combine(j):
        wait_all(y2_wait, j)
        both = []
        for k in range(NK):
            left = from_y[2 * k * YBLK:(2 * k + 1) * YBLK, chunk_cols(j)].astype(F32)
            right = from_y[(2 * k + 1) * YBLK:(2 * k + 2) * YBLK, chunk_cols(j)].astype(F32)
            both.append((left + right).astype(BF))
        both = jnp.concatenate(both, axis=0)
        to_z[:, chunk_cols(j)] = jnp.dot(to_lines, both, preferred_element_type=F32).astype(BF)
        start_all(z2_copy, j)
        from_z[own_z, chunk_cols(j)] = to_z[own_z, chunk_cols(j)]

    def finish(j):
        wait_all(z2_wait, j)
        combined = from_z[:, chunk_cols(j)]
        total = jnp.dot(mix[0], combined, preferred_element_type=F32)
        total += jnp.dot(mix[1], combined, preferred_element_type=F32)
        total += jnp.dot(mix[2], combined, preferred_element_type=F32)
        out_ref[:, chunk_cols(j)] = total.astype(BF)

    wait_sibling(2, zh)
    down(0)
    down(1)
    pass_far(2, zo)
    combine(0)
    wait_sibling(2, zo)
    down(2)
    down(3)
    combine(1)
    combine(2)
    finish(0)
    combine(3)
    finish(1)
    finish(2)
    finish(3)

    for copy in sends:
        copy.wait_send()
    for h in (0, 1):
        sent_all(z1_copy, h)
        sent_all(y1_copy, h)
    for j in range(4):
        sent_all(y2_copy, j)
        sent_all(z2_copy, j)


def per_device(tokens, expert_ids, gate_values, capacity, w_in, w_down):
    dma = pltpu.SemaphoreType.DMA
    vmem = pl.BlockSpec(memory_space=pltpu.VMEM)
    hbm = pl.BlockSpec(memory_space=pl.ANY)
    call = pl.pallas_call(
        layer_kernel,
        out_shape=jax.ShapeDtypeStruct(tokens.shape, BF),
        in_specs=[hbm, vmem, vmem, vmem, hbm, hbm],
        out_specs=vmem,
        scratch_shapes=[
            pltpu.VMEM((128, 2048), BF),
            pltpu.VMEM((128, 2048), BF),
            pltpu.VMEM((128, 2048), BF),
            pltpu.VMEM((128, 2048), BF),
            pltpu.VMEM((256, 2048), BF),
            pltpu.VMEM((2048, 1024), BF),
            pltpu.VMEM((16, 512, 128), BF),
            pltpu.VMEM((128, 1024), BF),
            pltpu.VMEM((512, 128), BF),
            pltpu.VMEM((256, 1024), F32),
            pltpu.VMEM((256, 512), BF),
            pltpu.VMEM((256, 2048), BF),
            pltpu.VMEM((256, 2048), BF),
            pltpu.VMEM((128, 2048), BF),
            pltpu.VMEM((128, 2048), BF),
            pltpu.VMEM((3, 128, 128), BF),
            dma((3,)),
            dma((2, 8)), dma((2, 8)), dma((2, 8)), dma((2, 8)),
            dma((3, 16)), dma((3, 16)), dma((3,)),
            dma((4, 8)), dma((4, 8)), dma((4, 8)), dma((4, 8)),
        ],
        compiler_params=pltpu.CompilerParams(
            collective_id=0, has_side_effects=True, vmem_limit_bytes=40 * 1024 * 1024
        ),
        name="expert_layer",
    )
    return call(
        tokens,
        expert_ids.T,
        gate_values.T,
        capacity.reshape(1, -1),
        w_in[0],
        w_down[0],
    )


def solution(mesh):
    return jax.shard_map(
        per_device,
        mesh=mesh,
        in_specs=(
            P(("dp", "expert"), None),
            P(("dp", "expert"), None),
            P(("dp", "expert"), None),
            P(),
            P("expert", "dp", None),
            P("expert", None, "dp"),
        ),
        out_specs=P(("dp", "expert"), None),
        check_vma=False,
    )
```

time: 334 us -> 132 us (0.40)
  waiting for transfers between devices: 223 us -> 0 us
  Pallas kernels: 0 us -> 125 us
  blocking collectives: 58.8 us -> 0 us
  starting transfers between devices: 22.6 us -> 0 us
  between operations: 13.5 us -> 0.02 us
  matrix products: 7.46 us -> 0 us
  other arithmetic: 3.43 us -> 0 us
    all_gather x2 -> x0, waiting for transfers between devices: 160 us -> none  [the longest x1 88.3 us: per_device(): lax.all_gather(local_down, 'dp', axis=1, tiled=True)]
    pallas_call x0 -> x1, Pallas kernels: none -> 125 us  [per_device(): call(tokens, expert_ids.T, gate_values.T, capacity.reshape(1, -1), w_in[0...]
    all_to_all x1 -> x0, waiting for transfers between devices: 61.6 us -> none  [per_device(): lax.all_to_all(doubled.reshape(2 * window, CAP, width), 'expert', split_a...]
    all_to_all x1 -> x0, blocking collectives: 58.8 us -> none  [per_device(): lax.all_to_all(partial_value, 'expert', split_axis=0, concat_axis=0, tile...]
    all_to_all x1 -> x0, starting transfers between devices: 22.5 us -> none  [per_device(): lax.all_to_all(doubled.reshape(2 * window, CAP, width), 'expert', split_a...]
    dot_general x4 -> x0, matrix products: 7.46 us -> none  [the longest x1 3.43 us: per_device(): jnp.dot(token_rows, lax.all_gather(local_in, 'dp', axis=0, tiled=True), p...]
    unnamed x3 -> x13, local copies, waits for them, and re-layouts: 0.79 us -> 4.38 us
  transfers between devices with their start and end apart: 3 -> 0, of which waited for: 3 -> 0; matrix products, arithmetic and copies ran while one was open for 3% -> 0% of each run, Pallas kernels for 0% -> 0%
where the time goes in v1:
time: 132 us; the launch traced here: 130 us
  Pallas kernels  125 us (95%)
  local copies, waits for them, and re-layouts  4.38 us (3%)
    pallas_call x1, Pallas kernels, per_device(): call(tokens, expert_ids.T, gate_values.T, capacity.reshape(1, -1), w_in[0...  125 us
    unnamed x13, local copies, waits for them, and re-layouts  4.38 us

profile of v1, /device:TPU:1, one launch (start us, length us, event | category | flops | bytes accessed | tf_op | source)
XLA Modules:
  0.0 129.9 jit_solution(7018867385521381025)
XLA Ops:
  0.0 0.0 copy-start.4
  0.0 0.0 copy-start.3
  0.0 0.0 copy-start.5
  0.0 0.7 copy-done.4
  0.7 0.0 copy-done.3
  0.7 0.0 copy-done.5
  0.7 0.0 copy-start
  0.7 1.0 copy-done
  1.7 0.0 copy-start.1
  1.7 0.9 copy-done.1
  2.7 0.0 copy-start.2
  2.7 0.9 copy-done.2
  3.6 125.5 %expert_layer.1 = bf16[128,2048]{1,0:T(8,128)(2,1)S(1)} custom-call(bf16[128,2048]{1,0:T(8,128)(2,1)S(1)} %copy-done, s32[2,128]{1,0:T(2,128)S(1)} %bitcast.7, f32[2,128]{1,0:T(2,128)S(1)} %bitcast.8, s32[1,32]{1,0:T(1,128)S(1)} %bitcast.9, bf16[128,1024]{1,0:T(8,128)(2,1)S(1)} %bitcast.5, bf16[512,128]{1,0:T(8,128)(2,1)S(1)} %bitcast.6), custom_call_target="tpu_custom_call" | custom-call | tf_op jit(solution)/shard_map/expert_layer/pallas_call | solution.py:454
  129.1 0.8 copy.8
Async XLA Ops:
  0.0 0.7 copy-start.4
  0.0 0.7 copy-start.3
  0.0 0.7 copy-start.5
  0.7 1.0 copy-start
  1.7 0.9 copy-start.1
  2.7 0.9 copy-start.2
